TPU v7x, 256 devices: a whole 4x4x8 slice. The times are simulated.
256 devices in a mesh: section: 4 (over y), chan: 64 (over x, z, core).
Axes of the slice: x: 4, y: 4, z: 8, core: 2. Of those that a mesh axis runs over, the one named last changes fastest.
Arguments:
- voltages: bfloat16 [2, 1024, 16, 4096], P(None, 'chan', 'section'), may hold values from -6 to 6
- coefficients: float32 [4, 4096], replicated, may hold values from -0.046875 to 0.046875
- tile_order: int32 [64, 36], P('chan'), may hold values from 0 to 35, each once within a row
- steer_table: bfloat16 [256, 2, 512], replicated, may hold values from -0.1875 to 0.1875
- beam_index: int32 [256, 64], P(None, 'chan'), may hold values from 0 to 255
Outputs:
- visibility: float32 [64, 36, 2, 128, 128], P('chan', 'section')
- beam_power: float32 [2, 256, 16, 4096], P(None, None, 'section', 'chan')
Inputs may be any that keep to these rules, and one draw needn't show every extreme that they name: Row g of tile_order lists each of the 36 work items of channel column g exactly once.
All inputs are finite; a program needn't handle non-finite values.
Results may differ from a plain program's by a relative error of at most 0.0029.
Values may be sent and summed in bfloat16 or wider, within the bound.
A program may use at most 64 MiB of HBM per device.

v0:
```python
import math
import jax
import jax.numpy as jnp
from jax import lax
from jax.sharding import PartitionSpec as P

STATIONS = 512
INPUTS = 1024
NA = 64
NB = 64
AVG = 64
TB = 128
PAIRS = 36
NBEAM = 256


def shifted(value, axis, by):
    devices = lax.axis_size(axis)
    pairs = [(i, i + by) for i in range(devices) if 0 <= i + by < devices]
    return lax.ppermute(value, axis, pairs)


def dft_table(length):
    counter = lax.iota(jnp.int32, length)
    phases = counter[:, None] * counter[None, :] % length
    angles = 2.0 * math.pi / length * phases.astype(jnp.float32)
    cosine = jnp.cos(angles)
    sine_part = jnp.sin(angles)
    return jnp.stack([jnp.stack([cosine, -sine_part]), jnp.stack([sine_part, cosine])])


def channelize(filtered):
    spectra_count = filtered.shape[1]
    length = NA * NB
    blocks = filtered.reshape(2, spectra_count, NA, NB)
    section_one = jnp.einsum("qmab,qrac->rmcb", blocks, dft_table(NA), precision=lax.Precision.HIGH)
    row_index = lax.iota(jnp.int32, NA)
    col_index = lax.iota(jnp.int32, NB)
    angles = (
        2.0
        * math.pi
        / length
        * (row_index[:, None] * col_index[None, :] % length).astype(jnp.float32)
    )
    cosine = jnp.cos(angles)
    sine_part = jnp.sin(angles)
    turned_real = section_one[0] * cosine + section_one[1] * sine_part
    turned_imag = section_one[1] * cosine - section_one[0] * sine_part
    twisted = jnp.stack([turned_real, turned_imag])
    section_two = jnp.einsum(
        "rmcb,rsbd->smdc", twisted, dft_table(NB), precision=lax.Precision.HIGH
    )
    return section_two.reshape(2, spectra_count, length)


def pair_products(spectra, work_items):
    tile_count = INPUTS // TB
    local_channel = work_items // PAIRS
    pair_number = work_items % PAIRS
    tile_ids = lax.iota(jnp.int32, tile_count)
    first_pairs = tile_ids * (tile_ids + 1) // 2
    row_tiles = (
        jnp.sum((first_pairs[None, :] <= pair_number[:, None]).astype(jnp.int32), axis=1) - 1
    )
    col_tiles = pair_number - row_tiles * (row_tiles + 1) // 2
    frame_count = spectra.shape[2]
    channel_groups = spectra.shape[3] // AVG
    blocks = spectra.reshape(2, tile_count, TB, frame_count, channel_groups, AVG)
    tile_table = jnp.transpose(blocks, (1, 4, 0, 2, 3, 5)).reshape(
        tile_count * channel_groups, 2, TB, frame_count * AVG
    )
    row_block = jnp.take(tile_table, row_tiles * channel_groups + local_channel, axis=0)
    col_block = jnp.take(tile_table, col_tiles * channel_groups + local_channel, axis=0)
    swapped = jnp.stack([row_block[:, 1], -row_block[:, 0]], axis=1)
    numbers = (((1, 3), (1, 3)), ((0,), (0,)))
    real_part = lax.dot_general(row_block, col_block, numbers, preferred_element_type=jnp.float32)
    imag_part = lax.dot_general(swapped, col_block, numbers, preferred_element_type=jnp.float32)
    return jnp.stack([real_part, imag_part], axis=1)


def shards(voltages, coefficients, tile_order, steer_table, beam_index):
    section_count = lax.axis_size("section")
    inputs_dev = voltages.shape[1]
    frames_dev = voltages.shape[2]
    tap_count = coefficients.shape[0]
    history = shifted(voltages[:, :, frames_dev - (tap_count - 1) :, :], "section", 1)
    extended = jnp.concatenate([history, voltages], axis=2).astype(jnp.float32)
    filtered = jnp.zeros(voltages.shape, jnp.float32)
    for tap_index in range(tap_count):
        offset = tap_count - 1 - tap_index
        filtered = (
            filtered + coefficients[tap_index] * extended[:, :, offset : offset + frames_dev, :]
        )
    spectra = (
        channelize(filtered.reshape(2, inputs_dev * frames_dev, NA * NB))
        .reshape(voltages.shape)
        .astype(jnp.bfloat16)
    )
    weights = steer_table[beam_index]
    out_dev = beam_index.shape[1]
    shard_piece = lax.all_to_all(spectra, "chan", split_axis=3, concat_axis=1, tiled=True)
    frame_count = shard_piece.shape[2]
    grouped = shard_piece.reshape(2, STATIONS, 2, frame_count, out_dev, AVG)
    product = lax.dot_general(
        weights, grouped, (((3,), (1,)), ((1,), (4,))), preferred_element_type=jnp.float32
    )
    real_part = product[:, :, 0, 0] - product[:, :, 1, 1]
    imag_part = product[:, :, 0, 1] + product[:, :, 1, 0]
    beam_energy = real_part * real_part + imag_part * imag_part
    beam_power = jnp.transpose(beam_energy, (2, 1, 3, 0, 4)).reshape(
        2, NBEAM, frame_count, out_dev * AVG
    )
    column_items = tile_order[0]
    items_dev = column_items.shape[0] // section_count
    mean_factor = 1.0 / (frames_dev * section_count * AVG)
    own_items = lax.dynamic_slice_in_dim(
        column_items, lax.axis_index("section") * items_dev, items_dev
    )
    totals = pair_products(lax.all_gather(shard_piece, "section", axis=2, tiled=True), own_items)
    visibility = (totals * mean_factor)[None]
    return (visibility, beam_power)


def solution(mesh):
    placed = (P(None, "chan", "section", None), P(), P("chan", None), P(), P(None, "chan"))
    return jax.shard_map(
        shards,
        mesh=mesh,
        in_specs=placed,
        out_specs=(P("chan", "section", None, None, None), P(None, None, "section", "chan")),
        check_vma=False,
    )
```

profile of v0, /device:TPU:1, one launch (start us, length us, event | category | flops | bytes accessed | tf_op | source)
XLA Modules:
  0.0 257.8 jit_solution(14299678543089905093)
XLA Ops:
  7.2 1.9 slice.54
  9.7 4.1 %collective-permute-start = (bf16[2,16,3,4096]{3,1,2,0:T(8,128)(2,1)S(1)}, bf16[2,16,3,4096]{3,1,2,0:T(8,128)(2,1)S(1)}, u32[]{:S(2)}, u32[]{:S(2)}) collective-permute-start(bf16[2,16,3,4096]{3,1,2,0:T(8,128)(2,1)S(1)} %copy.79), channel_id=1, source_target_pairs={{0,64},{64,128},{128,192},{1,65},{65,129},{129,193},{2,66},{66,130... | collective-permute-start | bytes 2359304 | tf_op jit(solution)/shard_map/ppermute | solution.py:20
  14.4 15.6 %collective-permute-done = bf16[2,16,3,4096]{3,1,2,0:T(8,128)(2,1)S(1)} collective-permute-done((bf16[2,16,3,4096]{3,1,2,0:T(8,128)(2,1)S(1)}, bf16[2,16,3,4096]{3,1,2,0:T(8,128)(2,1)S(1)}, u32[]{:S(2)}, u32[]{:S(2)}) %collective-permute-start) | collective-permute-done | bytes 786464 | tf_op jit(solution)/shard_map/ppermute | solution.py:20
  31.7 1.8 fusion.14
  33.5 3.3 %reshape_reshape.4 = f32[2,64,64,64]{3,2,1,0:T(8,128)} reshape(f32[2,16,4,4096]{3,2,1,0:T(4,128)S(1)} %fusion.14) | data formatting | bytes 4194304 | tf_op jit(solution)/shard_map/reshape;reshape | solution.py:35
  36.9 4.2 %fusion.10 = f32[2,64,64,64]{3,2,1,0:T(8,128)S(1)} fusion(f32[2,64,64,64]{3,2,1,0:T(8,128)} %reshape_reshape.4, f32[1,2,64,64]{2,3,0,1:T(8,128)S(1)} %get-tuple-element.27, f32[1,2,64,64]{2,3,0,1:T(8,128)S(1)} %get-tuple-element.26), kind=kOutput, calls=%fused_computation.18 | convolution fusion | flops 402669568 | bytes 4259840 | tf_op jit(solution)/shard_map/qmab,qrac->rmcb/dot_general | solution.py:36
  42.0 3.3 %fusion.13 = bf16[2,64,64,64]{3,2,1,0:T(8,128)(2,1)S(1)} fusion(f32[1,2,64,64]{2,3,0,1:T(8,128)S(1)} %get-tuple-element.27, f32[1,2,64,64]{2,3,0,1:T(8,128)S(1)} %get-tuple-element.26, f32[1,64,64,64]{3,2,1,0:T(8,128)S(1)} %get-tuple-element.21, f32[1,64,64,64]{3,2,1,0:T(8,128)S(1)} %get-tuple-element.20), kind=kOutput, calls=%fused_computation.19 | convolution fusion | flops 403718144 | bytes 3211264 | tf_op jit(solution)/shard_map/rmcb,rsbd->smdc/dot_general | solution.py:50
  45.3 2.2 convert_element_type.61
  47.5 12.0 %copy.55 = bf16[2,16,4,4096]{1,2,0,3:T(4,128)(2,1)} copy(bf16[2,16,4,4096]{3,2,1,0:T(4,128)(2,1)} %convert_element_type.61) | data formatting | bytes 2097152 | tf_op jit(solution)/shard_map/convert_element_type | solution.py:97
  59.5 11.9 %reshape.317 = bf16[64,2,4096]{2,1,0:T(2,128)(2,1)S(1)} reshape(bf16[4096,2,4,16]{3,2,1,0:T(4,128)(2,1)} %bitcast.95) | data formatting | bytes 2097152
  71.4 41.3 %all_to_all.18 = bf16[64,2,4096]{2,1,0:T(2,128)(2,1)S(1)} all-to-all(bf16[64,2,4096]{2,1,0:T(2,128)(2,1)S(1)} %reshape.317), channel_id=1, replica_groups=mesh['section'=4,'chan'=64] {'chan'}, dimensions={0} | all-to-all | bytes 2097152 | tf_op jit(solution)/shard_map/all_to_all | solution.py:101
  112.7 7.5 %reshape.318 = bf16[4096,2,4,16]{3,2,1,0:T(4,128)(2,1)} reshape(bf16[64,2,4096]{2,1,0:T(2,128)(2,1)S(1)} %all_to_all.18) | data formatting | bytes 2097152
  120.3 11.4 %copy.75 = bf16[2,16,4,64,64]{4,1,3,2,0:T(8,128)(2,1)} copy(bf16[2,16,4,64,64]{1,2,0,4,3:T(4,128)(2,1)} %bitcast.94) | data formatting | bytes 2097152 | tf_op jit(solution)/shard_map/all_to_all | solution.py:101
  131.7 1.7 gather_fusion
  133.9 3.5 %copy.64 = bf16[2,512,2,4,64]{1,4,3,2,0:T(8,128)(2,1)} copy(bf16[2,512,2,4,64]{4,2,1,3,0:T(2,128)(2,1)S(1)} %bitcast.97) | data formatting | bytes 2097152 | tf_op jit(solution)/shard_map/reshape.8
  137.4 2.0 convolution_bitcast_fusion
  140.3 74.9 %all-gather.2.cloned.1.call-done = bf16[2,1024,16,64]{3,1,2,0:T(8,128)(2,1)} async-done(((bf16[2,1024,4,64]{3,1,2,0:T(8,128)(2,1)}), bf16[2,1024,16,64]{3,1,2,0:T(8,128)(2,1)}) %all-gather.2.cloned.1.call-update) | async-done | bytes 4194320 | tf_op jit(solution)/shard_map/all_gather | solution.py:119
  215.2 8.6 %copy.58 = bf16[2,8,128,16,1,64]{2,5,3,0,1,4:T(8,128)(2,1)} copy(bf16[2,8,128,16,1,64]{5,2,1,3,0,4:T(8,128)(2,1)} %bitcast.98) | data formatting | bytes 8388608 | tf_op jit(solution)/shard_map/reshape | solution.py:68
  223.8 6.5 %copy.59 = bf16[8,2,128,1024]{3,2,1,0:T(8,128)(2,1)} copy(bf16[8,2,128,1024]{2,3,1,0:T(8,128)(2,1)} %bitcast.92) | data formatting | bytes 8388608 | tf_op jit(solution)/shard_map/reshape | solution.py:69
  230.3 5.8 %gather_fusion.2 = bf16[9,2,128,1024]{2,3,1,0:T(8,128)(2,1)} fusion(bf16[8,2,128,1024]{2,3,1,0:T(8,128)(2,1)} %bitcast.93, s32[1024]{0:T(1024)S(1)} %pad_clamp_fusion.1), kind=kCustom, calls=%fused_computation.1.clone | custom fusion | bytes 9437220 | tf_op jit(solution)/shard_map/jit(_take)/gather | solution.py:73
  236.1 5.8 %gather_fusion.1 = bf16[9,2,128,1024]{3,2,1,0:T(8,128)(2,1)} fusion(bf16[8,2,128,1024]{3,2,1,0:T(8,128)(2,1)} %copy.59, s32[1024]{0:T(1024)S(1)} %pad_clamp_fusion.2), kind=kCustom, calls=%fused_computation.clone | custom fusion | bytes 9437220 | tf_op jit(solution)/shard_map/jit(_take)/gather | solution.py:72
  242.0 3.0 %broadcast_select_fusion.1 = bf16[9,2,128,1024]{3,2,1,0:T(8,128)(2,1)S(1)} fusion(bf16[9,2,128,1024]{3,2,1,0:T(8,128)(2,1)} %gather_fusion.1, pred[9]{0:T(512)(128)(4,1)S(1)} %get-tuple-element.13), kind=kLoop, calls=%fused_computation.8 | loop fusion | flops 2359296 | bytes 9437193 | tf_op jit(solution)/shard_map/jit(_take)/select_n | solution.py:72
  246.2 1.5 fusion.20
  247.6 2.0 fusion.21
  (43 shorter events, 7.6 us)
Async XLA Ops:
  7.2 124.6 %copy-start = (bf16[256,2,512]{2,1,0:T(2,128)(2,1)S(1)}, bf16[256,2,512]{2,1,0:T(2,128)(2,1)}, u32[]{:S(2)}) copy-start(bf16[256,2,512]{2,1,0:T(2,128)(2,1)} %param.10) | copy-start | bytes 1572868
  7.2 7.1 %copy-start.4 = (f32[4,4096]{1,0:T(4,128)S(1)}, f32[4,4096]{1,0:T(4,128)}, u32[]{:S(2)}) copy-start(f32[4,4096]{1,0:T(4,128)} %param.8) | copy-start | bytes 196612
  7.2 208.1 %all-gather.2.cloned.1.call-start = ((), (), s32[]{:S(2)}) async-start(), calls=%async_computation.1 | async-start | bytes 10485760 | tf_op jit(solution)/shard_map/all_gather | solution.py:119
  9.1 21.5 %copy-start.3 = (bf16[2,16,4,4096]{3,2,1,0:T(4,128)(2,1)S(1)}, bf16[2,16,4,4096]{3,2,1,0:T(4,128)(2,1)}, u32[]{:S(2)}) copy-start(bf16[2,16,4,4096]{3,2,1,0:T(4,128)(2,1)} %param.7) | copy-start | bytes 3145732
  9.7 20.2 %collective-permute-start = (bf16[2,16,3,4096]{3,1,2,0:T(8,128)(2,1)S(1)}, bf16[2,16,3,4096]{3,1,2,0:T(8,128)(2,1)S(1)}, u32[]{:S(2)}, u32[]{:S(2)}) collective-permute-start(bf16[2,16,3,4096]{3,1,2,0:T(8,128)(2,1)S(1)} %copy.79), channel_id=1, source_target_pairs={{0,64},{64,128},{128,192},{1,65},{65,129},{129,193},{2,66},{66,130... | collective-permute-start | bytes 2359304 | tf_op jit(solution)/shard_map/ppermute | solution.py:20
  120.3 11.4 %copy-start.6 = (s32[256,1]{0,1:T(1,128)S(1)}, s32[256,1]{0,1:T(1,128)}, u32[]{:S(2)}) copy-start(s32[256,1]{0,1:T(1,128)} %param.11) | copy-start | bytes 3076
  131.6 1.8 copy-start.5
  131.6 2.2 copy-start.2
  242.0 3.6 %slice-start = ((s8[4718592]{0:T(1024)(128)(4,1)}), s8[4194304]{0:T(1024)(128)(4,1)S(1)}, s32[]{:S(2)}) async-start(s8[4718592]{0:T(1024)(128)(4,1)} %bitcast.99), calls=%async_computation.2 | async-start | bytes 8388608
  245.0 1.2 slice-start.1
  247.6 3.3 %copy-start.1 = (bf16[256,2,512]{2,1,0:T(2,128)(2,1)S(1)}, bf16[256,2,512]{2,1,0:T(2,128)(2,1)}, u32[]{:S(2)}) copy-start(bf16[256,2,512]{2,1,0:T(2,128)(2,1)} %param.10) | copy-start | bytes 1572868
Sparse Core Ops, SparseCore 0:
  131.8 83.4 all-gather.1
where the time goes:
time: 259 us; the launch traced here: 258 us
  waiting for transfers between devices  90.6 us (35%)
  local copies, waits for them, and re-layouts  85.5 us (33%)
  blocking collectives  41.3 us (16%)
  between operations  14.3 us (6%)
  matrix products  12.9 us (5%)
  other arithmetic  9 us (3%)
  starting transfers between devices  4.11 us (2%)
    all_gather x1, waiting for transfers between devices, shards(): lax.all_gather(shard_piece, 'section', axis=2, tiled=True)  74.9 us
    all_to_all x1, blocking collectives, shards(): lax.all_to_all(spectra, 'chan', split_axis=3, concat_axis=1, tiled=True)  41.3 us
    unnamed x22, local copies, waits for them, and re-layouts  22.1 us
    ppermute x1, waiting for transfers between devices, shifted(): return lax.ppermute(value, axis, pairs)  15.6 us
    convert_element_type x2, local copies, waits for them, and re-layouts, shards(): spectra = channelize(filtered.reshape(2, inputs_dev * frames_dev, NA * NB...  14.2 us
    all_to_all x1, local copies, waits for them, and re-layouts, shards(): lax.all_to_all(spectra, 'chan', split_axis=3, concat_axis=1, tiled=True)  11.4 us
    reshape x1, local copies, waits for them, and re-layouts, pair_products(): spectra.reshape(2, tile_count, TB, frame_count, channel_groups, AVG)  8.56 us
    reshape x1, local copies, waits for them, and re-layouts, pair_products(): jnp.transpose(blocks, (1, 4, 0, 2, 3, 5))  6.46 us
  transfers between devices with their start and end apart: 2, of which 2 were waited for; matrix products, arithmetic and copies ran while one was open for 4% of the time, Pallas kernels for 0%

commit v1 on v0

--- a/solution.py
+++ b/solution.py
@@ -12,6 +12,27 @@
 TB = 128
 PAIRS = 36
 NBEAM = 256
+
+
+def gather_around(x, axis, dim):
+    length, mine, rows = (lax.axis_size(axis), lax.axis_index(axis), x.shape[dim])
+    right = [(i, (i + 1) % length) for i in range(length)]
+    behind = [(i, (i - 1) % length) for i in range(length)]
+    whole = jnp.zeros((*x.shape[:dim], length * rows, *x.shape[dim + 1 :]), x.dtype)
+    whole = lax.dynamic_update_slice_in_dim(whole, x, mine * rows, axis=dim)
+    from_left = from_right = x
+    half = length // 2
+    for step in range(1, half + 1):
+        from_left = lax.ppermute(from_left, axis, right)
+        whole = lax.dynamic_update_slice_in_dim(
+            whole, from_left, (mine - step) % length * rows, axis=dim
+        )
+        if step < length - half:
+            from_right = lax.ppermute(from_right, axis, behind)
+            whole = lax.dynamic_update_slice_in_dim(
+                whole, from_right, (mine + step) % length * rows, axis=dim
+            )
+    return whole
 
 
 def shifted(value, axis, by):
@@ -116,7 +137,7 @@
     own_items = lax.dynamic_slice_in_dim(
         column_items, lax.axis_index("section") * items_dev, items_dev
     )
-    totals = pair_products(lax.all_gather(shard_piece, "section", axis=2, tiled=True), own_items)
+    totals = pair_products(gather_around(shard_piece, "section", 2), own_items)
     visibility = (totals * mean_factor)[None]
     return (visibility, beam_power)
 

time: 259 us -> 224 us (0.86)
  waiting for transfers between devices: 90.6 us -> 53.3 us
  between operations: 14.3 us -> 0.99 us
  local copies, waits for them, and re-layouts: 85.5 us -> 92.7 us
  starting transfers between devices: 4.11 us -> 7.78 us
  matrix products: 12.9 us -> 15.6 us
    all_gather x1 -> x0, waiting for transfers between devices: 74.9 us -> none  [shards(): lax.all_gather(shard_piece, 'section', axis=2, tiled=True)]
    ppermute x0 -> x3, waiting for transfers between devices: none -> 37.7 us  [the longest x2 37.7 us: gather_around(): from_left = lax.ppermute(from_left, axis, right)]
    reshape x1 -> x0, local copies, waits for them, and re-layouts: 8.56 us -> none  [pair_products(): spectra.reshape(2, tile_count, TB, frame_count, channel_groups, AVG)]
    transpose x0 -> x1, local copies, waits for them, and re-layouts: none -> 5.41 us  [pair_products(): jnp.transpose(blocks, (1, 4, 0, 2, 3, 5))]
    unnamed x22 -> x27, local copies, waits for them, and re-layouts: 22.1 us -> 26.6 us
    dynamic_update_slice x0 -> x4, local copies, waits for them, and re-layouts: none -> 4.03 us  [the longest x2 2.62 us: gather_around(): lax.dynamic_update_slice_in_dim(whole, from_left, (mine - step) % length...]
    dot_general x1, matrix products: 1.46 us -> 5.35 us  [pair_products(): lax.dot_general(row_block, col_block, numbers, preferred_element_type=jnp...]
    ppermute x0 -> x3, starting transfers between devices: none -> 3.71 us  [the longest x2 2.21 us: gather_around(): from_left = lax.ppermute(from_left, axis, right)]
  transfers between devices with their start and end apart: 2 -> 4, of which waited for: 2 -> 3; matrix products, arithmetic and copies ran while one was open for 4% -> 5% of each run, Pallas kernels for 0% -> 0%
where the time goes in v1:
time: 224 us; the launch traced here: 222 us
  local copies, waits for them, and re-layouts  92.7 us (41%)
  waiting for transfers between devices  53.3 us (24%)
  blocking collectives  41.3 us (18%)
  matrix products  15.6 us (7%)
  other arithmetic  10.5 us (5%)
  starting transfers between devices  7.78 us (3%)
    all_to_all x1, blocking collectives, shards(): lax.all_to_all(spectra, 'chan', split_axis=3, concat_axis=1, tiled=True)  41.3 us
    ppermute x2, waiting for transfers between devices, gather_around(): from_left = lax.ppermute(from_left, axis, right)  37.7 us
    unnamed x27, local copies, waits for them, and re-layouts  26.6 us
    ppermute x1, waiting for transfers between devices, shifted(): return lax.ppermute(value, axis, pairs)  15.6 us
    convert_element_type x2, local copies, waits for them, and re-layouts, shards(): spectra = channelize(filtered.reshape(2, inputs_dev * frames_dev, NA * NB...  14.2 us
    all_to_all x2, local copies, waits for them, and re-layouts, shards(): lax.all_to_all(spectra, 'chan', split_axis=3, concat_axis=1, tiled=True)  12.2 us
    reshape x1, local copies, waits for them, and re-layouts, pair_products(): jnp.transpose(blocks, (1, 4, 0, 2, 3, 5))  6.77 us
    gather x1, local copies, waits for them, and re-layouts, pair_products(): jnp.take(tile_table, col_tiles * channel_groups + local_channel, axis=0)  5.92 us
  transfers between devices with their start and end apart: 4, of which 3 were waited for; matrix products, arithmetic and copies ran while one was open for 5% of the time, Pallas kernels for 0%

profile of v1, /device:TPU:1, one launch (start us, length us, event | category | flops | bytes accessed | tf_op | source)
XLA Modules:
  0.0 222.1 jit_solution(4254572561794098069)
XLA Ops:
  0.7 2.0 slice.54
  3.2 4.1 %collective-permute-start = (bf16[2,16,3,4096]{3,1,2,0:T(8,128)(2,1)S(1)}, bf16[2,16,3,4096]{3,1,2,0:T(8,128)(2,1)S(1)}, u32[]{:S(2)}, u32[]{:S(2)}) collective-permute-start(bf16[2,16,3,4096]{3,1,2,0:T(8,128)(2,1)S(1)} %copy.89), channel_id=1, source_target_pairs={{0,64},{64,128},{128,192},{1,65},{65,129},{129,193},{2,66},{66,130... | collective-permute-start | bytes 2359304 | tf_op jit(solution)/shard_map/ppermute | solution.py:41
  7.8 15.6 %collective-permute-done = bf16[2,16,3,4096]{3,1,2,0:T(8,128)(2,1)S(1)} collective-permute-done((bf16[2,16,3,4096]{3,1,2,0:T(8,128)(2,1)S(1)}, bf16[2,16,3,4096]{3,1,2,0:T(8,128)(2,1)S(1)}, u32[]{:S(2)}, u32[]{:S(2)}) %collective-permute-start) | collective-permute-done | bytes 786464 | tf_op jit(solution)/shard_map/ppermute | solution.py:41
  27.0 3.3 %reshape_reshape.4 = f32[2,64,64,64]{3,2,1,0:T(8,128)} reshape(f32[2,16,4,4096]{3,2,1,0:T(4,128)S(1)} %fusion.14) | data formatting | bytes 4194304 | tf_op jit(solution)/shard_map/reshape;reshape | solution.py:56
  30.4 4.2 %fusion.10 = f32[2,64,64,64]{3,2,1,0:T(8,128)S(1)} fusion(f32[2,64,64,64]{3,2,1,0:T(8,128)} %reshape_reshape.4, f32[1,2,64,64]{2,3,0,1:T(8,128)S(1)} %get-tuple-element.27, f32[1,2,64,64]{2,3,0,1:T(8,128)S(1)} %get-tuple-element.26), kind=kOutput, calls=%fused_computation.18 | convolution fusion | flops 402669568 | bytes 4259840 | tf_op jit(solution)/shard_map/qmab,qrac->rmcb/dot_general | solution.py:57
  35.5 3.3 %fusion.13 = bf16[2,64,64,64]{3,2,1,0:T(8,128)(2,1)S(1)} fusion(f32[1,2,64,64]{2,3,0,1:T(8,128)S(1)} %get-tuple-element.27, f32[1,2,64,64]{2,3,0,1:T(8,128)S(1)} %get-tuple-element.26, f32[1,64,64,64]{3,2,1,0:T(8,128)S(1)} %get-tuple-element.21, f32[1,64,64,64]{3,2,1,0:T(8,128)S(1)} %get-tuple-element.20), kind=kOutput, calls=%fused_computation.19 | convolution fusion | flops 403718144 | bytes 3211264 | tf_op jit(solution)/shard_map/rmcb,rsbd->smdc/dot_general | solution.py:71
  38.8 2.2 convert_element_type.61
  41.0 12.0 %copy.61 = bf16[2,16,4,4096]{1,2,0,3:T(4,128)(2,1)} copy(bf16[2,16,4,4096]{3,2,1,0:T(4,128)(2,1)} %convert_element_type.61) | data formatting | bytes 2097152 | tf_op jit(solution)/shard_map/convert_element_type | solution.py:118
  53.0 11.9 %reshape.317 = bf16[64,2,4096]{2,1,0:T(2,128)(2,1)S(1)} reshape(bf16[4096,2,4,16]{3,2,1,0:T(4,128)(2,1)} %bitcast.104) | data formatting | bytes 2097152
  64.9 41.3 %all_to_all.18 = bf16[64,2,4096]{2,1,0:T(2,128)(2,1)S(1)} all-to-all(bf16[64,2,4096]{2,1,0:T(2,128)(2,1)S(1)} %reshape.317), channel_id=1, replica_groups=mesh['section'=4,'chan'=64] {'chan'}, dimensions={0} | all-to-all | bytes 2097152 | tf_op jit(solution)/shard_map/all_to_all | solution.py:122
  106.2 7.5 %reshape.318 = bf16[4096,2,4,16]{3,2,1,0:T(4,128)(2,1)} reshape(bf16[64,2,4096]{2,1,0:T(2,128)(2,1)S(1)} %all_to_all.18) | data formatting | bytes 2097152
  113.8 10.6 %copy.84 = bf16[2,16,4,64,64]{4,1,3,2,0:T(8,128)(2,1)S(1)} copy(bf16[2,16,4,64,64]{1,2,0,4,3:T(4,128)(2,1)} %bitcast.103) | data formatting | bytes 2097152 | tf_op jit(solution)/shard_map/all_to_all | solution.py:122
  126.0 2.2 collective-permute-start.1
  130.1 23.3 %collective-permute-done.1 = bf16[2,1024,4,64]{1,3,2,0:T(8,128)(2,1)} collective-permute-done((bf16[2,1024,4,64]{1,3,2,0:T(8,128)(2,1)}, bf16[2,1024,4,64]{1,3,2,0:T(8,128)(2,1)}, u32[]{:S(2)}, u32[]{:S(2)}) %collective-permute-start.1) | collective-permute-done | bytes 1048608 | tf_op jit(solution)/shard_map/ppermute | solution.py:26
  155.3 3.5 %copy.73 = bf16[2,512,2,4,64]{1,4,3,2,0:T(8,128)(2,1)} copy(bf16[2,512,2,4,64]{4,2,1,3,0:T(2,128)(2,1)S(1)} %bitcast.107) | data formatting | bytes 2097152 | tf_op jit(solution)/shard_map/reshape.8
  164.6 14.4 %collective-permute-done.3 = bf16[2,1024,4,64]{1,3,2,0:T(8,128)(2,1)} collective-permute-done((bf16[2,1024,4,64]{1,3,2,0:T(8,128)(2,1)}, bf16[2,1024,4,64]{1,3,2,0:T(8,128)(2,1)}, u32[]{:S(2)}, u32[]{:S(2)}) %collective-permute-start.3) | collective-permute-done | bytes 1048608 | tf_op jit(solution)/shard_map/ppermute | solution.py:26
  180.3 3.0 %copy.90 = bf16[256,8,8,128]{3,2,1,0:T(8,128)(2,1)} copy(bf16[256,8,8,128]{3,1,2,0:T(8,128)(2,1)S(1)} %bitcast.108) | data formatting | bytes 8388608
  183.4 6.8 %copy.68 = bf16[8,2,128,1024]{3,2,1,0:T(8,128)(2,1)} copy(bf16[8,2,128,1024]{2,0,3,1:T(8,128)(2,1)} %bitcast.101) | data formatting | bytes 8388608 | tf_op jit(solution)/shard_map/reshape | solution.py:90
  190.1 5.4 %copy.67 = bf16[8,1,2,128,16,64]{3,5,4,2,0,1:T(8,128)(2,1)} copy(bf16[8,1,2,128,16,64]{3,0,5,4,2,1:T(8,128)(2,1)} %bitcast.102) | data formatting | bytes 8388608 | tf_op jit(solution)/shard_map/transpose | solution.py:90
  195.5 5.8 %gather_fusion.1 = bf16[9,2,128,1024]{3,2,1,0:T(8,128)(2,1)} fusion(bf16[8,2,128,1024]{3,2,1,0:T(8,128)(2,1)} %copy.68, s32[1024]{0:T(1024)S(1)} %pad_clamp_fusion.2), kind=kCustom, calls=%fused_computation.clone | custom fusion | bytes 9437220 | tf_op jit(solution)/shard_map/jit(_take)/gather | solution.py:93
  201.3 2.9 %broadcast_select_fusion.1 = bf16[9,2,128,1024]{3,2,1,0:T(8,128)(2,1)S(1)} fusion(bf16[9,2,128,1024]{3,2,1,0:T(8,128)(2,1)} %gather_fusion.1, pred[9]{0:T(512)(128)(4,1)S(1)} %get-tuple-element.13), kind=kLoop, calls=%fused_computation.8 | loop fusion | flops 2359296 | bytes 9437193 | tf_op jit(solution)/shard_map/jit(_take)/select_n | solution.py:93
  207.0 5.9 %gather_fusion.2 = bf16[9,2,128,1024]{2,3,1,0:T(8,128)(2,1)} fusion(bf16[8,2,128,1024]{2,3,1,0:T(8,128)(2,1)} %bitcast.105, s32[1024]{0:T(1024)S(1)} %pad_clamp_fusion.1), kind=kCustom, calls=%fused_computation.1.clone | custom fusion | bytes 9437220 | tf_op jit(solution)/shard_map/jit(_take)/gather | solution.py:94
  213.0 5.4 %fusion.20 = f32[1,9,1,128,128]{4,3,1,2,0:T(8,128)S(1)} fusion(bf16[9,2,128,1024]{3,2,1,0:T(8,128)(2,1)} %copy-done.2, bf16[9,2,128,1024]{2,3,1,0:T(8,128)(2,1)} %gather_fusion.2, pred[9]{0:T(512)(128)(4,1)S(1)} %get-tuple-element.16), kind=kOutput, calls=%fused_computation.32 | convolution fusion | flops 606339072 | bytes 10027017 | tf_op jit(solution)/shard_map/dot_general | solution.py:97
  218.8 2.0 fusion.21
  (56 shorter events, 22.6 us)
Async XLA Ops:
  0.6 152.9 %copy-start = (bf16[256,2,512]{2,1,0:T(2,128)(2,1)S(1)}, bf16[256,2,512]{2,1,0:T(2,128)(2,1)}, u32[]{:S(2)}) copy-start(bf16[256,2,512]{2,1,0:T(2,128)(2,1)} %param.10) | copy-start | bytes 1572868
  0.6 23.5 %copy-start.6 = (bf16[2,16,4,4096]{3,2,1,0:T(4,128)(2,1)S(1)}, bf16[2,16,4,4096]{3,2,1,0:T(4,128)(2,1)}, u32[]{:S(2)}) copy-start(bf16[2,16,4,4096]{3,2,1,0:T(4,128)(2,1)} %param.7) | copy-start | bytes 3145732
  0.7 7.1 %copy-start.8 = (f32[4,4096]{1,0:T(4,128)S(1)}, f32[4,4096]{1,0:T(4,128)}, u32[]{:S(2)}) copy-start(f32[4,4096]{1,0:T(4,128)} %param.8) | copy-start | bytes 196612
  3.2 20.2 %collective-permute-start = (bf16[2,16,3,4096]{3,1,2,0:T(8,128)(2,1)S(1)}, bf16[2,16,3,4096]{3,1,2,0:T(8,128)(2,1)S(1)}, u32[]{:S(2)}, u32[]{:S(2)}) collective-permute-start(bf16[2,16,3,4096]{3,1,2,0:T(8,128)(2,1)S(1)} %copy.89), channel_id=1, source_target_pairs={{0,64},{64,128},{128,192},{1,65},{65,129},{129,193},{2,66},{66,130... | collective-permute-start | bytes 2359304 | tf_op jit(solution)/shard_map/ppermute | solution.py:41
  113.8 14.5 %copy-start.9 = (s32[1,36]{1,0:T(1,128)S(1)}, s32[1,36]{1,0:T(1,128)}, u32[]{:S(2)}) copy-start(s32[1,36]{1,0:T(1,128)} %param.9) | copy-start | bytes 436
  113.8 14.6 %copy-start.10 = (s32[256,1]{0,1:T(1,128)S(1)}, s32[256,1]{0,1:T(1,128)}, u32[]{:S(2)}) copy-start(s32[256,1]{0,1:T(1,128)} %param.11) | copy-start | bytes 3076
  126.0 27.4 %collective-permute-start.1 = (bf16[2,1024,4,64]{1,3,2,0:T(8,128)(2,1)}, bf16[2,1024,4,64]{1,3,2,0:T(8,128)(2,1)}, u32[]{:S(2)}, u32[]{:S(2)}) collective-permute-start(bf16[2,1024,4,64]{1,3,2,0:T(8,128)(2,1)} %copy.64), channel_id=1, source_target_pairs={{0,64},{64,128},{128,192},{192,0},{1,65},{65,129},{129,193},{193,1... | collective-permute-start | bytes 3145736 | tf_op jit(solution)/shard_map/ppermute | solution.py:26
  128.6 34.7 %collective-permute-start.2 = (bf16[2,1024,4,64]{1,3,2,0:T(8,128)(2,1)}, bf16[2,1024,4,64]{1,3,2,0:T(8,128)(2,1)}, u32[]{:S(2)}, u32[]{:S(2)}) collective-permute-start(bf16[2,1024,4,64]{1,3,2,0:T(8,128)(2,1)} %copy.64), channel_id=1, source_target_pairs={{0,192},{64,0},{128,64},{192,128},{1,193},{65,1},{129,65},{193,129... | collective-permute-start | bytes 3145736 | tf_op jit(solution)/shard_map/ppermute | solution.py:31
  153.4 25.6 %collective-permute-start.3 = (bf16[2,1024,4,64]{1,3,2,0:T(8,128)(2,1)}, bf16[2,1024,4,64]{1,3,2,0:T(8,128)(2,1)}, u32[]{:S(2)}, u32[]{:S(2)}) collective-permute-start(bf16[2,1024,4,64]{1,3,2,0:T(8,128)(2,1)} %collective-permute-done.1), channel_id=1, source_target_pairs={{0,64},{64,128},{128,192},{192,0},{1,65},{65,129},{129,193},{193,1... | collective-permute-start | bytes 3145736 | tf_op jit(solution)/shard_map/ppermute | solution.py:26
  158.7 1.2 copy-start.5
  158.7 1.5 copy-start.4
  204.2 2.9 %copy-start.2 = (bf16[9,2,128,1024]{3,2,1,0:T(8,128)(2,1)}, bf16[9,2,128,1024]{3,2,1,0:T(8,128)(2,1)S(1)}, u32[]{:S(2)}) copy-start(bf16[9,2,128,1024]{3,2,1,0:T(8,128)(2,1)S(1)} %broadcast_select_fusion.1) | copy-start | bytes 14155780
  213.0 5.4 %copy-start.3 = (bf16[9,2,128,1024]{2,3,1,0:T(8,128)(2,1)S(1)}, bf16[9,2,128,1024]{2,3,1,0:T(8,128)(2,1)}, u32[]{:S(2)}) copy-start(bf16[9,2,128,1024]{2,3,1,0:T(8,128)(2,1)} %gather_fusion.2) | copy-start | bytes 14155780
  213.0 5.9 %copy-start.7 = (bf16[9,1,128,1024]{3,2,1,0:T(8,128)(2,1)S(1)}, bf16[9,1,128,1024]{3,2,1,0:T(8,128)(2,1)}, u32[]{:S(2)}) copy-start(bf16[9,1,128,1024]{3,2,1,0:T(8,128)(2,1)} %get-tuple-element.19) | copy-start | bytes 7077892
  218.8 3.2 %copy-start.1 = (bf16[256,2,512]{2,1,0:T(2,128)(2,1)S(1)}, bf16[256,2,512]{2,1,0:T(2,128)(2,1)}, u32[]{:S(2)}) copy-start(bf16[256,2,512]{2,1,0:T(2,128)(2,1)} %param.10) | copy-start | bytes 1572868
